TPU v7x, 128 devices: a whole 4x4x4 slice. The times are simulated.
128 devices in a mesh: grp: 8 (over x_hi, z), mem: 16 (over y, x_lo, core).
Axes of the slice: x: 4 (x_hi: 2, x_lo: 2; x = x_hi * 2 + x_lo), y: 4, z: 4, core: 2. Of those that a mesh axis runs over, the one named last changes fastest.
Arguments:
- candidates: bfloat16 [131072, 4096], P(('grp', 'mem')), may hold values from -1 to 1
- round_one: bfloat16 [8192, 4096], P(('grp', 'mem')), may hold values from -1 to 1
- counts: int32 [8, 16], P('grp', 'mem'), may hold values from 1 to 64, 384 in all within a row
- chosen: int32 [8, 128], P('grp'), may hold values from 0 to 383, as said below
Outputs:
- group_dist: float32 [131072], P(('grp', 'mem'))
- final_dist: float32 [131072], P(('grp', 'mem'))
Inputs may be any that keep to these rules, and one draw needn't show every extreme that they name: In each group the counts sum to 384, and some device of each group has exactly 64. `chosen`: within a group the 128 positions are distinct, each below 384.
All inputs are finite; a program needn't handle non-finite values.
Results may differ from a plain program's by a relative error of at most 0.0003.
Values may be sent and summed in bfloat16 or wider, within the bound.
A program may use at most 128 MiB of HBM per device.

v0:
```python
import jax
import jax.numpy as jnp
from jax import lax
from jax.sharding import PartitionSpec as P


def sq_norms(matrix):
    return jnp.sum(jnp.square(matrix.astype(jnp.float32)), axis=1)


def distances(cand_rows, cand_norm, center_rows):
    inner = lax.dot_general(
        cand_rows, center_rows, (((1,), (1,)), ((), ())), preferred_element_type=jnp.float32
    )
    return cand_norm[:, None] + sq_norms(center_rows)[None, :] - 2.0 * inner


def lookup(table, index_values):
    entries = jnp.arange(table.shape[0], dtype=jnp.int32)
    match = index_values[:, None] == entries[None, :]
    return jnp.sum(jnp.where(match, table[None, :], 0), axis=1)


def body(candidates, round_one, counts, chosen):
    mem_size = lax.axis_size("mem")
    my_index = lax.axis_index("mem")
    slot_max = round_one.shape[0]
    width = round_one.shape[1]
    picks_total = chosen.shape[1]
    group_counts = lax.all_gather(counts, "mem", axis=1, tiled=True)[0]
    offsets = jnp.cumsum(group_counts) - group_counts
    picked_ids = chosen[0]
    cand_norm = sq_norms(candidates)
    start_state = (
        jnp.full((candidates.shape[0],), jnp.inf, jnp.float32),
        jnp.zeros((picks_total, width), jnp.float32),
    )
    block_rows = lax.all_gather(round_one, "mem", axis=0, tiled=True)
    slot_ids = jnp.arange(block_rows.shape[0], dtype=jnp.int32)
    holder = slot_ids // slot_max
    within = slot_ids % slot_max
    usable = within < lookup(group_counts, holder)
    position = lookup(offsets, holder) + within
    gaps = distances(candidates, cand_norm, block_rows)
    gaps = jnp.where(usable[None, :], gaps, jnp.inf)
    nearest = jnp.minimum(start_state[0], jnp.min(gaps, axis=1))
    select = ((picked_ids[:, None] == position[None, :]) & usable[None, :]).astype(jnp.bfloat16)
    collected = jnp.dot(select, block_rows, preferred_element_type=jnp.float32)
    nearest, collected = (nearest, collected)
    picked = collected.astype(jnp.bfloat16)
    final_start = jnp.full((candidates.shape[0],), jnp.inf, jnp.float32)
    share = picks_total // mem_size
    my_share = lax.dynamic_slice_in_dim(picked, my_index * share, share, 0)
    final = jnp.minimum(
        final_start,
        jnp.min(
            distances(
                candidates, cand_norm, lax.all_gather(my_share, ("grp", "mem"), axis=0, tiled=True)
            ),
            axis=1,
        ),
    )
    return (nearest, final)


def solution(mesh):
    in_specs = (P(("grp", "mem"), None), P(("grp", "mem"), None), P("grp", "mem"), P("grp", None))
    out_specs = (P(("grp", "mem")), P(("grp", "mem")))
    return jax.shard_map(body, mesh=mesh, in_specs=in_specs, out_specs=out_specs, check_vma=False)
```

profile of v0, /device:TPU:1, one launch (start us, length us, event | category | flops | bytes accessed | tf_op | source)
XLA Modules:
  0.0 298.8 jit_solution(11337238122814754986)
XLA Ops:
  7.2 0.0 all-gather.3.cloned.1.call-start
  7.2 0.7 all-gather.3.cloned.1.call-update
  7.9 0.0 all-gather.5.cloned.1.call-start
  8.6 1.2 dynamic-slice
  9.8 0.7 bitcast_dynamic-update-slice_fusion
  10.5 11.0 %all-reduce = s32[16]{0:T(128)S(1)} all-reduce(s32[16]{0:T(128)S(1)} %bitcast_dynamic-update-slice_fusion), channel_id=1, replica_groups=mesh['grp'=8,'mem'=16] {'mem'}, use_global_device_ids=true, to_apply=%add | all-reduce | flops 16 | bytes 128
  21.5 0.2 reduce-window_clone.1
  21.7 0.1 select_reduce_fusion.1
  21.8 43.6 %all-gather.3.cloned.1.call-done = bf16[1024,4096]{1,0:T(8,128)(2,1)} async-done(((bf16[64,4096]{1,0:T(8,128)(2,1)}), bf16[1024,4096]{1,0:T(8,128)(2,1)}) %all-gather.3.cloned.1.call-update) | async-done | bytes 8388624 | tf_op jit(solution)/shard_map/all_gather | solution.py:38
  65.5 4.7 %fusion.1 = bf16[128,4096]{1,0:T(8,128)(2,1)S(1)} fusion(bf16[1024,4096]{1,0:T(8,128)(2,1)} %all-gather.3.cloned.1.call-done, s32[1024]{0:T(1024)S(1)} %fusion.10, s32[128]{0:T(128)} %bitcast.17, pred[1024]{0:T(1024)(128)(4,1)S(1)} %fusion.11), kind=kOutput, calls=%fused_computation.6 | convolution fusion | flops 1074003968 | bytes 9442816 | tf_op jit(solution)/shard_map/dot_general | solution.py:48
  70.2 0.6 dynamic-slice_convert_fusion
  70.8 0.0 all-gather.5.cloned.1.call-update
  70.8 0.0 copy-start
  70.8 5.2 %multiply_reduce_fusion.2 = f32[1024]{0:T(1024)S(1)} fusion(bf16[1024,4096]{1,0:T(8,128)(2,1)} %param.4), kind=kLoop, calls=%fused_computation.2 | loop fusion | flops 12581888 | bytes 8392704 | tf_op jit(solution)/shard_map/reduce_sum | solution.py:8
  76.1 0.5 copy-done
  76.6 1.7 multiply_reduce_fusion.1
  78.3 12.3 %select_reduce_fusion = f32[1024]{0:T(1024)} fusion(bf16[1024,4096]{1,0:T(8,128)(2,1)} %param.4, bf16[1024,4096]{1,0:T(8,128)(2,1)S(1)} %copy-done, f32[1024]{0:T(1024)S(1)} %multiply_reduce_fusion.1, f32[1024]{0:T(1024)S(1)} %multiply_reduce_fusion.2, pred[1024]{0:T(1024)(128)(4,1)S(1)} %fusion.11), kind=kOutput, calls=%fused_computation.5 | convolution fusion | flops 8595176448 | bytes 16790528 | tf_op jit(solution)/shard_map/dot_general | solution.py:12
  90.6 183.8 %all-gather.5.cloned.1.call-done = bf16[1024,4096]{1,0:T(8,128)(2,1)} async-done(((bf16[8,4096]{1,0:T(8,128)(2,1)}), bf16[1024,4096]{1,0:T(8,128)(2,1)}) %all-gather.5.cloned.1.call-update) | async-done | bytes 8388624 | tf_op jit(solution)/shard_map/all_gather | solution.py:58
  274.3 0.0 copy-start.1
  274.3 5.2 %multiply_reduce_fusion = f32[1024]{0:T(1024)S(1)} fusion(bf16[1024,4096]{1,0:T(8,128)(2,1)} %all-gather.5.cloned.1.call-done), kind=kLoop, calls=%fused_computation | loop fusion | flops 12581888 | bytes 8392704 | tf_op jit(solution)/shard_map/reduce_sum | solution.py:8
  279.5 0.5 copy-done.1
  280.1 11.9 %fusion = f32[1024]{0:T(1024)} fusion(bf16[1024,4096]{1,0:T(8,128)(2,1)S(1)} %copy-done.1, bf16[1024,4096]{1,0:T(8,128)(2,1)} %param.4, f32[1024]{0:T(1024)S(1)} %multiply_reduce_fusion, f32[1024]{0:T(1024)S(1)} %multiply_reduce_fusion.2), kind=kOutput, calls=%fused_computation.4 | convolution fusion | flops 8594127872 | bytes 16789504 | tf_op jit(solution)/shard_map/dot_general | solution.py:12
  (5 shorter events, 0.0 us)
Async XLA Ops:
  7.2 58.3 %all-gather.3.cloned.1.call-start = ((), (), s32[]{:S(2)}) async-start(), calls=%async_computation | async-start | bytes 8912896 | tf_op jit(solution)/shard_map/all_gather | solution.py:38
  7.9 266.4 %all-gather.5.cloned.1.call-start = ((), (), s32[]{:S(2)}) async-start(), calls=%async_computation.1 | async-start | bytes 8454144 | tf_op jit(solution)/shard_map/all_gather | solution.py:58
  70.8 5.8 %copy-start = (bf16[1024,4096]{1,0:T(8,128)(2,1)S(1)}, bf16[1024,4096]{1,0:T(8,128)(2,1)}, u32[]{:S(2)}) copy-start(bf16[1024,4096]{1,0:T(8,128)(2,1)} %all-gather.3.cloned.1.call-done) | copy-start | bytes 25165828
  274.3 5.8 %copy-start.1 = (bf16[1024,4096]{1,0:T(8,128)(2,1)S(1)}, bf16[1024,4096]{1,0:T(8,128)(2,1)}, u32[]{:S(2)}) copy-start(bf16[1024,4096]{1,0:T(8,128)(2,1)} %all-gather.5.cloned.1.call-done) | copy-start | bytes 25165828
Sparse Core Ops, SparseCore 0:
  9.7 55.7 all-gather.2
  70.9 203.3 all-gather.4
where the time goes:
time: 299 us
  waiting for transfers between devices  228 us (76%)
  matrix products  28.8 us (10%)
  between operations  14.7 us (5%)
  other arithmetic  12.4 us (4%)
  blocking collectives  11 us (4%)
  local copies, waits for them, and re-layouts  3.63 us (1%)
    all_gather x1, waiting for transfers between devices, body(): lax.all_gather(my_share, ('grp', 'mem'), axis=0, tiled=True)  184 us
    all_gather x1, waiting for transfers between devices, body(): block_rows = lax.all_gather(round_one, 'mem', axis=0, tiled=True)  43.6 us
    dot_general x2, matrix products, distances(): lax.dot_general(cand_rows, center_rows, (((1,), (1,)), ((), ())), preferr...  24.1 us
    reduce_sum x3, other arithmetic, sq_norms(): return jnp.sum(jnp.square(matrix.astype(jnp.float32)), axis=1)  12.1 us
    unnamed x1, blocking collectives  11 us
  transfers between devices with their start and end apart: 2, of which 2 were waited for; matrix products, arithmetic and copies ran while one was open for 7% of the time, Pallas kernels for 0%

commit v1 on v0

--- a/solution.py
+++ b/solution.py
@@ -2,6 +2,13 @@
 import jax.numpy as jnp
 from jax import lax
 from jax.sharding import PartitionSpec as P
+
+
+def all_by_exchange(array, axis, dim):
+    count = lax.axis_size(axis)
+    blocks = jnp.stack([array for _ in range(count)])
+    blocks = lax.all_to_all(blocks, axis, split_axis=0, concat_axis=0)
+    return jnp.concatenate(blocks, axis=dim)
 
 
 def sq_norms(matrix):
@@ -54,10 +61,7 @@
     final = jnp.minimum(
         final_start,
         jnp.min(
-            distances(
-                candidates, cand_norm, lax.all_gather(my_share, ("grp", "mem"), axis=0, tiled=True)
-            ),
-            axis=1,
+            distances(candidates, cand_norm, all_by_exchange(my_share, ("grp", "mem"), 0)), axis=1
         ),
     )
     return (nearest, final)

time: 299 us -> 220 us (0.74)
  the two profiles are of different devices: /device:TPU:1 before, /device:TPU:14 now
where the time goes in v1:
time: 220 us; the launch traced here: 219 us
  waiting for transfers between devices  131 us (60%)
  matrix products  31.4 us (14%)
  other arithmetic  15.8 us (7%)
  between operations  14.8 us (7%)
  blocking collectives  10.5 us (5%)
  starting transfers between devices  9.7 us (4%)
  local copies, waits for them, and re-layouts  6.3 us (3%)
    all_to_all x1, waiting for transfers between devices, all_by_exchange(): blocks = lax.all_to_all(blocks, axis, split_axis=0, concat_axis=0)  87.5 us
    all_gather x1, waiting for transfers between devices, body(): block_rows = lax.all_gather(round_one, 'mem', axis=0, tiled=True)  42.7 us
    dot_general x2, matrix products, distances(): lax.dot_general(cand_rows, center_rows, (((1,), (1,)), ((), ())), preferr...  26.7 us
    reduce_sum x3, other arithmetic, sq_norms(): return jnp.sum(jnp.square(matrix.astype(jnp.float32)), axis=1)  15.5 us
    unnamed x1, blocking collectives  10.5 us
    all_to_all x1, starting transfers between devices, all_by_exchange(): blocks = lax.all_to_all(blocks, axis, split_axis=0, concat_axis=0)  9.66 us
    dot_general x1, matrix products, body(): collected = jnp.dot(select, block_rows, preferred_element_type=jnp.float32)  4.69 us
  transfers between devices with their start and end apart: 2, of which 2 were waited for; matrix products, arithmetic and copies ran while one was open for 11% of the time, Pallas kernels for 0%

profile of v1, /device:TPU:14, one launch (start us, length us, event | category | flops | bytes accessed | tf_op | source)
XLA Modules:
  0.0 219.3 jit_solution(16794981724334185637)
XLA Ops:
  7.2 0.0 all-gather.2.cloned.1.call-start
  7.2 0.7 all-gather.2.cloned.1.call-update
  8.5 1.2 dynamic-slice
  9.8 0.7 bitcast_dynamic-update-slice_fusion
  10.5 10.5 %all-reduce = s32[16]{0:T(128)S(1)} all-reduce(s32[16]{0:T(128)S(1)} %bitcast_dynamic-update-slice_fusion), channel_id=1, replica_groups=mesh['grp'=8,'mem'=16] {'mem'}, use_global_device_ids=true, to_apply=%add | all-reduce | flops 16 | bytes 128
  21.0 0.2 reduce-window_clone.1
  21.2 0.1 select_reduce_fusion.1
  21.3 42.7 %all-gather.2.cloned.1.call-done = bf16[1024,4096]{1,0:T(8,128)(2,1)} async-done(((bf16[64,4096]{1,0:T(8,128)(2,1)}), bf16[1024,4096]{1,0:T(8,128)(2,1)}) %all-gather.2.cloned.1.call-update) | async-done | bytes 8388624 | tf_op jit(solution)/shard_map/all_gather | solution.py:45
  64.0 4.7 %fusion.5 = bf16[128,4096]{1,0:T(8,128)(2,1)S(1)} fusion(bf16[1024,4096]{1,0:T(8,128)(2,1)} %all-gather.2.cloned.1.call-done, s32[1024]{0:T(1024)S(1)} %fusion.14, s32[128]{0:T(128)} %bitcast.23, pred[1024]{0:T(1024)(128)(4,1)S(1)} %fusion.15), kind=kOutput, calls=%fused_computation.8 | convolution fusion | flops 1074003968 | bytes 9442816 | tf_op jit(solution)/shard_map/dot_general | solution.py:55
  68.7 4.3 %stack.2 = bf16[128,8,4096]{2,1,0:T(8,128)(2,1)} broadcast(bf16[8,4096]{1,0:T(8,128)(2,1)S(1)} %dynamic-slice_convert_fusion), dimensions={1,2} | broadcast | bytes 8454144 | tf_op jit(solution)/shard_map/stack | solution.py:9
  73.0 9.7 %all-to-all-start = ((bf16[128,8,4096]{2,1,0:T(8,128)(2,1)}), bf16[128,8,4096]{2,1,0:T(8,128)(2,1)}, u32[]{:S(2)}, u32[]{:S(2)}) async-start(bf16[128,8,4096]{2,1,0:T(8,128)(2,1)} %stack.2), calls=%async_computation | async-start | bytes 16777216 | tf_op jit(solution)/shard_map/all_to_all | solution.py:10
  82.6 0.0 slice-start
  82.6 5.2 %multiply_reduce_fusion.2 = f32[1024]{0:T(1024)S(1)} fusion(bf16[1024,4096]{1,0:T(8,128)(2,1)} %param.4), kind=kLoop, calls=%fused_computation.2 | loop fusion | flops 12581888 | bytes 8392704 | tf_op jit(solution)/shard_map/reduce_sum | solution.py:15
  87.9 0.0 slice-start.1
  87.9 5.2 %multiply_reduce_fusion.1 = f32[1024]{0:T(1024)S(1)} fusion(bf16[1024,4096]{1,0:T(8,128)(2,1)} %all-gather.2.cloned.1.call-done), kind=kLoop, calls=%fused_computation.1 | loop fusion | flops 12581888 | bytes 8392704 | tf_op jit(solution)/shard_map/reduce_sum | solution.py:15
  93.1 0.0 slice-done
  93.1 0.0 slice-done.1
  93.1 12.1 %select_reduce_fusion = f32[1024]{0:T(1024)} fusion(bf16[1024,4096]{1,0:T(8,128)(2,1)} %param.4, bf16[1024,4096]{1,0:T(8,128)(2,1)S(1)} %bitcast.22, f32[1024]{0:T(1024)S(1)} %multiply_reduce_fusion.1, f32[1024]{0:T(1024)S(1)} %multiply_reduce_fusion.2, pred[1024]{0:T(1024)(128)(4,1)S(1)} %fusion.15), kind=kOutput, calls=%fused_computation.7 | convolution fusion | flops 8595176448 | bytes 16790528 | tf_op jit(solution)/shard_map/dot_general | solution.py:19
  105.2 87.5 %all-to-all-done = bf16[128,8,4096]{2,1,0:T(8,128)(2,1)} async-done(((bf16[128,8,4096]{2,1,0:T(8,128)(2,1)}), bf16[128,8,4096]{2,1,0:T(8,128)(2,1)}, u32[]{:S(2)}, u32[]{:S(2)}) %all-to-all-start) | async-done | bytes 8388640 | tf_op jit(solution)/shard_map/all_to_all | solution.py:10
  192.7 5.1 %multiply_reduce_fusion = f32[128,8]{1,0:T(8,128)S(1)} fusion(bf16[128,8,4096]{2,1,0:T(8,128)(2,1)} %all-to-all-done), kind=kLoop, calls=%fused_computation | loop fusion | flops 12581888 | bytes 8392704 | tf_op jit(solution)/shard_map/reduce_sum | solution.py:15
  197.8 0.1 add.62
  197.9 14.6 %fusion.2 = f32[1024]{0:T(1024)} fusion(bf16[1024,4096]{1,0:T(8,128)(2,1)} %param.4, bf16[128,8,4096]{2,1,0:T(8,128)(2,1)} %all-to-all-done, f32[1024]{0:T(1024)S(1)} %add.62, f32[1024]{0:T(1024)S(1)} %multiply_reduce_fusion.2), kind=kOutput, calls=%fused_computation.6 | convolution fusion | flops 8594127872 | bytes 16789504 | tf_op jit(solution)/shard_map/dot_general | solution.py:19
  (7 shorter events, 0.0 us)
Async XLA Ops:
  7.2 56.8 %all-gather.2.cloned.1.call-start = ((), (), s32[]{:S(2)}) async-start(), calls=%async_computation.1 | async-start | bytes 8912896 | tf_op jit(solution)/shard_map/all_gather | solution.py:45
  73.0 119.7 %all-to-all-start = ((bf16[128,8,4096]{2,1,0:T(8,128)(2,1)}), bf16[128,8,4096]{2,1,0:T(8,128)(2,1)}, u32[]{:S(2)}, u32[]{:S(2)}) async-start(bf16[128,8,4096]{2,1,0:T(8,128)(2,1)} %stack.2), calls=%async_computation | async-start | bytes 16777216 | tf_op jit(solution)/shard_map/all_to_all | solution.py:10
  82.6 10.5 %slice-start = ((s8[8388608]{0:T(1024)(128)(4,1)}), s8[4194304]{0:T(1024)(128)(4,1)S(1)}, s32[]{:S(2)}) async-start(s8[8388608]{0:T(1024)(128)(4,1)} %bitcast.21), calls=%async_computation.2 | async-start | bytes 8388608
  87.9 5.2 %slice-start.1 = ((s8[8388608]{0:T(1024)(128)(4,1)}), s8[4194304]{0:T(1024)(128)(4,1)S(1)}, s32[]{:S(2)}) async-start(s8[8388608]{0:T(1024)(128)(4,1)} %bitcast.21), calls=%async_computation.3 | async-start | bytes 8388608
Sparse Core Ops, SparseCore 0:
  9.7 54.2 all-gather.1
